TPU v7x, 256 devices: a whole 4x4x8 slice. The times are simulated.
256 devices in a mesh: blk: 32 (over x_lo, z, core), slab: 8 (over x_hi, y).
Axes of the slice: x: 4 (x_hi: 2, x_lo: 2; x = x_hi * 2 + x_lo), y: 4, z: 8, core: 2. Of those that a mesh axis runs over, the one named last changes fastest.
Arguments:
- tokens: bfloat16 [4194304, 128], P(('blk', 'slab')), may hold values from -6 to 6
- listed: int32 [16384, 3], P(('blk', 'slab')), may hold values from 0 to 1023, as said below
- centroids: bfloat16 [262144, 128], P('blk'), may hold values from -6 to 6
Outputs:
- refined: float32 [262144, 128], P(('blk', 'slab'))
- counts: float32 [262144], P(('blk', 'slab'))
Inputs may be any that keep to these rules, and one draw needn't show every extreme that they name: `listed`: in the rows of one device (64 token blocks), all ids of one owner group (id // 32) are equal, so a device names at most one block of each owner group. The three ids of a row are distinct.
All inputs are finite; a program needn't handle non-finite values.
Results may differ from a plain program's by a relative error of at most 0.00093.
Values may be sent and summed in bfloat16 or wider, within the bound.
No kernel may reach another device: no remote copies, remote signals or barrier semaphores. Data moves between devices by JAX's collectives and lax.ppermute only.
A program may use at most 128 MiB of HBM per device.

v0:
```python
import jax
import jax.numpy as jnp
from jax import lax
from jax.sharding import PartitionSpec as P

EMBED_WIDTH = 128
CENT_BLK = 256
TOK_BLK = 256
BPO = 32


SOFTMAX_TEMP = 0.1
PRIOR_WEIGHT = 4.0
EPSILON = 1e-06


def unit_rows(values):
    widened = values.astype(jnp.float32)
    return widened * lax.rsqrt(jnp.mean(widened * widened, axis=-1, keepdims=True) + EPSILON)


def finish_sums(back_sums, back_counts, asked_ids):
    slab_number_count = lax.axis_size("slab")
    slab_index = lax.axis_index("slab")
    pick_rows = (asked_ids[:, None] == jnp.arange(BPO, dtype=jnp.int32)).astype(jnp.float32)
    own_sums = jnp.einsum("js,jcd->scd", pick_rows, back_sums, precision=lax.Precision.HIGHEST)
    own_counts = jnp.einsum("js,jc->sc", pick_rows, back_counts, precision=lax.Precision.HIGHEST)
    share_blocks = BPO // slab_number_count
    total_sums, total_counts = lax.psum((own_sums, own_counts), "slab")
    mine_sums = lax.dynamic_slice_in_dim(total_sums, slab_index * share_blocks, share_blocks, 0)
    mine_counts = lax.dynamic_slice_in_dim(total_counts, slab_index * share_blocks, share_blocks, 0)
    return (mine_sums, mine_counts)


def shards(tokens, listed, centroids):
    owner_count = lax.axis_size("blk")
    slab_number_count = lax.axis_size("slab")
    slab_index = lax.axis_index("slab")
    centroid_norm = unit_rows(centroids).reshape(BPO, CENT_BLK, EMBED_WIDTH)
    cent_send = centroid_norm.astype(jnp.bfloat16)
    tok_norm = unit_rows(tokens).astype(jnp.bfloat16).reshape(-1, TOK_BLK, EMBED_WIDTH)
    block_count = tok_norm.shape[0]
    owner_ids = jnp.arange(owner_count, dtype=jnp.int32)
    group_of = listed // BPO
    inner_ids = listed % BPO
    matches = group_of[:, :, None] == owner_ids
    wanted = jnp.max(jnp.where(matches, inner_ids[:, :, None] + 1, 0), axis=(0, 1)) - 1
    request_rows = lax.all_gather(wanted.reshape(1, owner_count), "blk", axis=0, tiled=True)
    asked_ids = lax.dynamic_index_in_dim(request_rows, lax.axis_index("blk"), 1, keepdims=False)
    replies = cent_send[jnp.maximum(asked_ids, 0)]
    fetched = lax.all_to_all(replies, "blk", split_axis=0, concat_axis=0, tiled=True)
    group_size = min(16, block_count)
    turn_count = block_count // group_size

    def accumulate(state_pair, turn_index):
        sum_acc, count_acc = state_pair
        start = turn_index * group_size
        token_rows = lax.dynamic_slice_in_dim(tok_norm, start, group_size, 0)
        slot_ids = lax.dynamic_slice_in_dim(group_of, start, group_size, 0)
        candidate_centroids = fetched[slot_ids].reshape(group_size, 3 * CENT_BLK, EMBED_WIDTH)
        score_matrix = jnp.einsum(
            "wsy,way->wsa", token_rows, candidate_centroids, preferred_element_type=jnp.float32
        ) / (EMBED_WIDTH * SOFTMAX_TEMP)
        weights = jnp.exp(score_matrix)
        weights = weights / jnp.sum(weights, axis=-1, keepdims=True)
        weights_low = weights.astype(jnp.bfloat16).reshape(group_size, TOK_BLK, 3, CENT_BLK)
        partial_value = jnp.einsum(
            "gtkc,gtd->gkcd", weights_low, token_rows, preferred_element_type=jnp.float32
        )
        part_counts = jnp.sum(weights.reshape(group_size, TOK_BLK, 3, CENT_BLK), axis=1)
        one_hot = (slot_ids.reshape(-1)[:, None] == owner_ids).astype(jnp.float32)
        sum_acc = sum_acc + jnp.einsum(
            "ns,ncd->scd",
            one_hot,
            partial_value.reshape(-1, CENT_BLK, EMBED_WIDTH),
            precision=lax.Precision.HIGHEST,
        )
        count_acc = count_acc + jnp.einsum(
            "ns,nc->sc", one_hot, part_counts.reshape(-1, CENT_BLK), precision=lax.Precision.HIGHEST
        )
        return ((sum_acc, count_acc), None)

    start_pair = (
        jnp.zeros((owner_count, CENT_BLK, EMBED_WIDTH), jnp.float32),
        jnp.zeros((owner_count, CENT_BLK), jnp.float32),
    )
    (sum_acc, count_acc), _ = lax.scan(
        accumulate, start_pair, jnp.arange(turn_count, dtype=jnp.int32)
    )
    back_sums, back_counts = (
        lax.all_to_all(sum_acc, "blk", split_axis=0, concat_axis=0, tiled=True),
        lax.all_to_all(count_acc, "blk", split_axis=0, concat_axis=0, tiled=True),
    )
    mine_sums, mine_counts = finish_sums(back_sums, back_counts, asked_ids)
    share_blocks = BPO // slab_number_count
    mine_cent = lax.dynamic_slice_in_dim(centroid_norm, slab_index * share_blocks, share_blocks, 0)
    refined = (mine_sums + PRIOR_WEIGHT * mine_cent) / (mine_counts[:, :, None] + PRIOR_WEIGHT)
    return (
        refined.reshape(share_blocks * CENT_BLK, EMBED_WIDTH),
        mine_counts.reshape(share_blocks * CENT_BLK),
    )


def solution(mesh):
    placed = (P(("blk", "slab"), None), P(("blk", "slab"), None), P("blk", None))
    return jax.shard_map(
        shards,
        mesh=mesh,
        in_specs=placed,
        out_specs=(P(("blk", "slab"), None), P(("blk", "slab"))),
        check_vma=False,
    )
```

profile of v0, /device:TPU:1, one launch (start us, length us, event | category | flops | bytes accessed | tf_op | source)
XLA Modules:
  0.0 573.2 jit_solution(4882123108803830461)
XLA Ops:
  7.2 0.7 fusion.35
  7.9 1.3 dynamic-slice
  9.8 0.1 select_reduce_fusion
  9.9 0.1 add_dynamic-update-slice_fusion
  10.1 107.6 %all-reduce.1 = s32[32,32]{1,0:T(8,128)S(1)} all-reduce(s32[32,32]{1,0:T(8,128)S(1)} %reshape.90), channel_id=2, replica_groups=mesh['blk'=32,'slab'=8] {'blk'}, use_global_device_ids=true, to_apply=%add | all-reduce | flops 1024 | bytes 8192
  117.7 0.2 dynamic-slice_reduce_fusion
  117.9 2.7 fusion.23
  120.7 4.6 convert_multiply_fusion.2
  125.3 1.9 copy-done.2
  127.2 0.3 convert_element_type.20
  127.6 2.2 gather_fusion.1
  129.7 8.1 %all-to-all-start = ((bf16[32,256,128]{2,1,0:T(8,128)(2,1)}), bf16[32,256,128]{2,1,0:T(8,128)(2,1)S(1)}, u32[]{:S(2)}, u32[]{:S(2)}) async-start(bf16[32,256,128]{2,1,0:T(8,128)(2,1)} %gather_fusion.1), calls=%async_computation | async-start | bytes 4194304 | tf_op jit(solution)/shard_map/all_to_all | solution.py:51
  137.8 0.2 all-reduce.4.cloned.1.call-start
  138.1 4.1 fusion.21
  142.2 7.8 %fusion.22 = bf16[16384,128]{1,0:T(8,128)(2,1)} fusion(bf16[16384,128]{1,0:T(8,128)(2,1)S(1)} %copy-done.3, f32[16384]{0:T(1024)S(1)} %add_rsqrt_fusion), kind=kLoop, calls=%fused_computation.29 | loop fusion | flops 6291456 | bytes 8454144 | tf_op jit(solution)/shard_map/convert_element_type | solution.py:41
  150.0 37.2 %all-to-all-done = bf16[32,256,128]{2,1,0:T(8,128)(2,1)S(1)} async-done(((bf16[32,256,128]{2,1,0:T(8,128)(2,1)}), bf16[32,256,128]{2,1,0:T(8,128)(2,1)S(1)}, u32[]{:S(2)}, u32[]{:S(2)}) %all-to-all-start) | async-done | bytes 2097184 | tf_op jit(solution)/shard_map/all_to_all | solution.py:51
  187.2 151.2 %while.13 = (s32[]{:T(128)}, f32[32,256,128]{2,0,1:T(8,128)}, f32[32,256]{1,0:T(8,128)S(1)}, s32[4]{0:T(128)S(1)}, s32[64,3]{0,1:T(4,128)S(1)}, /*index=5*/bf16[...) while((s32[]{:T(128)}, f32[32,256,128]{2,0,1:T(8,128)}, ...), condition=%wide.region_6.7_spmd.clone, body=%wide.region_3.6_spmd.clone.sunk | while | flops 2240286720 | bytes 99916664 | solution.py:87
  187.2 0.7 dynamic_slice.52
  188.9 2.7 gather_fusion
  191.7 3.4 fusion.55
  195.1 4.9 fusion.56
  200.0 8.6 %copy.88 = bf16[16,256,768]{1,2,0:T(8,128)(2,1)} copy(bf16[16,256,768]{2,1,0:T(8,128)(2,1)} %get-tuple-element.160) | data formatting | bytes 12582912 | tf_op jit(solution)/shard_map/while/body/eval_jaxpr/convert_element_type | solution.py:66
  208.6 4.8 fusion.57
  213.5 10.0 %select_add_fusion.2 = f32[32,256,128]{2,0,1:T(8,128)} fusion(f32[32,256,128]{2,0,1:T(8,128)} %get-tuple-element.174, f32[48,256,128]{2,1,0:T(8,128)S(1)} %bitcast.47, pred[]{:T(512)S(6)} %compare.6, s32[48]{0:T(128)S(1)} %eq.103), kind=kOutput, calls=%fused_computation.8.clone.1 | convolution fusion | flops 606078464 | bytes 14680257 | tf_op jit(solution)/shard_map/while/body/eval_jaxpr/ns,ncd->scd/dot_general | solution.py:72
  223.5 0.1 convolution_add_fusion.2
  223.7 0.7 dynamic_slice.52
  225.2 0.1 eq.103
  225.4 2.7 gather_fusion
  228.2 3.4 fusion.55
  231.5 4.9 fusion.56
  236.5 8.6 %copy.88 = bf16[16,256,768]{1,2,0:T(8,128)(2,1)} copy(bf16[16,256,768]{2,1,0:T(8,128)(2,1)} %get-tuple-element.160) | data formatting | bytes 12582912 | tf_op jit(solution)/shard_map/while/body/eval_jaxpr/convert_element_type | solution.py:66
  245.1 4.8 fusion.57
  250.0 11.7 %select_add_fusion.2 = f32[32,256,128]{2,0,1:T(8,128)} fusion(f32[32,256,128]{2,0,1:T(8,128)} %get-tuple-element.174, f32[48,256,128]{2,1,0:T(8,128)S(1)} %bitcast.47, pred[]{:T(512)S(6)} %compare.6, s32[48]{0:T(128)S(1)} %eq.103), kind=kOutput, calls=%fused_computation.8.clone.1 | convolution fusion | flops 606078464 | bytes 14680257 | tf_op jit(solution)/shard_map/while/body/eval_jaxpr/ns,ncd->scd/dot_general | solution.py:72
  261.7 0.1 convolution_add_fusion.2
  261.9 0.7 dynamic_slice.52
  263.6 2.7 gather_fusion
  266.3 3.4 fusion.55
  269.7 4.9 fusion.56
  274.7 8.6 %copy.88 = bf16[16,256,768]{1,2,0:T(8,128)(2,1)} copy(bf16[16,256,768]{2,1,0:T(8,128)(2,1)} %get-tuple-element.160) | data formatting | bytes 12582912 | tf_op jit(solution)/shard_map/while/body/eval_jaxpr/convert_element_type | solution.py:66
  283.3 4.8 fusion.57
  288.1 11.7 %select_add_fusion.2 = f32[32,256,128]{2,0,1:T(8,128)} fusion(f32[32,256,128]{2,0,1:T(8,128)} %get-tuple-element.174, f32[48,256,128]{2,1,0:T(8,128)S(1)} %bitcast.47, pred[]{:T(512)S(6)} %compare.6, s32[48]{0:T(128)S(1)} %eq.103), kind=kOutput, calls=%fused_computation.8.clone.1 | convolution fusion | flops 606078464 | bytes 14680257 | tf_op jit(solution)/shard_map/while/body/eval_jaxpr/ns,ncd->scd/dot_general | solution.py:72
  299.8 0.1 convolution_add_fusion.2
  300.0 0.7 dynamic_slice.52
  301.8 2.7 gather_fusion
  304.5 3.4 fusion.55
  307.9 4.9 fusion.56
  312.8 8.6 %copy.88 = bf16[16,256,768]{1,2,0:T(8,128)(2,1)} copy(bf16[16,256,768]{2,1,0:T(8,128)(2,1)} %get-tuple-element.160) | data formatting | bytes 12582912 | tf_op jit(solution)/shard_map/while/body/eval_jaxpr/convert_element_type | solution.py:66
  321.4 4.8 fusion.57
  326.3 11.7 %select_add_fusion.2 = f32[32,256,128]{2,0,1:T(8,128)} fusion(f32[32,256,128]{2,0,1:T(8,128)} %get-tuple-element.174, f32[48,256,128]{2,1,0:T(8,128)S(1)} %bitcast.47, pred[]{:T(512)S(6)} %compare.6, s32[48]{0:T(128)S(1)} %eq.103), kind=kOutput, calls=%fused_computation.8.clone.1 | convolution fusion | flops 606078464 | bytes 14680257 | tf_op jit(solution)/shard_map/while/body/eval_jaxpr/ns,ncd->scd/dot_general | solution.py:72
  338.0 0.1 convolution_add_fusion.2
  338.4 4.6 copy.58
  343.0 99.4 %all_to_all.22 = f32[32,256,128]{2,1,0:T(8,128)S(1)} all-to-all(f32[32,256,128]{2,1,0:T(8,128)S(1)} %copy.58), channel_id=1, replica_groups=mesh['blk'=32,'slab'=8] {'blk'}, dimensions={0} | all-to-all | bytes 8388608 | tf_op jit(solution)/shard_map/all_to_all | solution.py:91
  442.4 6.7 %fusion.24 = f32[32,256,128]{2,0,1:T(8,128)} fusion(f32[32,256,128]{2,1,0:T(8,128)S(1)} %all_to_all.22, s32[32]{0:T(128)S(1)} %get-tuple-element.87), kind=kOutput, calls=%fused_computation.33 | convolution fusion | flops 402654208 | bytes 8388736 | tf_op jit(solution)/shard_map/js,jcd->scd/dot_general | solution.py:26
  449.1 0.6 all_to_all.16
  449.7 5.9 %all-to-all-start.2 = ((f32[32,1,256]{2,1,0:T(1,128)}), f32[32,1,256]{2,1,0:T(1,128)S(1)}, u32[]{:S(2)}, u32[]{:S(2)}) async-start(f32[32,1,256]{2,1,0:T(1,128)} %all_to_all.16), calls=%async_computation.2 | async-start | bytes 65536 | tf_op jit(solution)/shard_map/all_to_all | solution.py:92
  455.7 1.1 constant_dynamic-slice_fusion.1
  456.7 6.8 %all-to-all-done.2 = f32[32,1,256]{2,1,0:T(1,128)S(1)} async-done(((f32[32,1,256]{2,1,0:T(1,128)}), f32[32,1,256]{2,1,0:T(1,128)S(1)}, u32[]{:S(2)}, u32[]{:S(2)}) %all-to-all-start.2) | async-done | bytes 32800 | tf_op jit(solution)/shard_map/all_to_all | solution.py:92
  463.6 0.1 fusion.28
  463.7 37.7 %psum.15 = f32[32,256]{1,0:T(8,128)S(1)} all-reduce(f32[32,256]{1,0:T(8,128)S(1)} %fusion.28), channel_id=1, replica_groups=mesh['blk'=32,'slab'=8] {'slab'}, use_global_device_ids=true, to_apply=%region_8.9 | all-reduce | flops 8192 | bytes 65536 | tf_op jit(solution)/shard_map/psum | solution.py:29
  501.4 0.6 copy.67
  502.0 0.1 copy.61
  502.2 61.6 %all-reduce.4.cloned.1.call-done = f32[32,256,128]{2,0,1:T(8,128)} async-done(((f32[32,256,128]{2,0,1:T(8,128)}), f32[32,256,128]{2,0,1:T(8,128)}) %all-reduce.4.cloned.1.call-update) | async-done | bytes 4194320 | tf_op jit(solution)/shard_map/psum | solution.py:29
  563.8 1.7 fusion.27
  565.5 0.8 copy.62
  (56 shorter events, 1.5 us)
Async XLA Ops:
  125.3 2.0 copy-start.2
  129.7 57.5 %all-to-all-start = ((bf16[32,256,128]{2,1,0:T(8,128)(2,1)}), bf16[32,256,128]{2,1,0:T(8,128)(2,1)S(1)}, u32[]{:S(2)}, u32[]{:S(2)}) async-start(bf16[32,256,128]{2,1,0:T(8,128)(2,1)} %gather_fusion.1), calls=%async_computation | async-start | bytes 4194304 | tf_op jit(solution)/shard_map/all_to_all | solution.py:51
  137.8 426.0 %all-reduce.4.cloned.1.call-start = ((), (), s32[]{:S(2)}) async-start(), calls=%async_computation.3 | async-start | bytes 8388608 | tf_op jit(solution)/shard_map/psum | solution.py:29
  138.1 4.1 copy-start.3
  187.2 1.7 copy-start
  213.5 10.2 %copy-start.1 = (bf16[32,256,128]{2,1,0:T(8,128)(2,1)S(1)}, bf16[32,256,128]{2,1,0:T(8,128)(2,1)}, u32[]{:S(2)}) copy-start(bf16[32,256,128]{2,1,0:T(8,128)(2,1)} %copy-done) | copy-start | bytes 6291460 | tf_op jit(solution)/shard_map/while
  223.7 1.7 copy-start
  249.9 11.9 %copy-start.1 = (bf16[32,256,128]{2,1,0:T(8,128)(2,1)S(1)}, bf16[32,256,128]{2,1,0:T(8,128)(2,1)}, u32[]{:S(2)}) copy-start(bf16[32,256,128]{2,1,0:T(8,128)(2,1)} %copy-done) | copy-start | bytes 6291460 | tf_op jit(solution)/shard_map/while
  261.8 1.7 copy-start
  288.1 11.9 %copy-start.1 = (bf16[32,256,128]{2,1,0:T(8,128)(2,1)S(1)}, bf16[32,256,128]{2,1,0:T(8,128)(2,1)}, u32[]{:S(2)}) copy-start(bf16[32,256,128]{2,1,0:T(8,128)(2,1)} %copy-done) | copy-start | bytes 6291460 | tf_op jit(solution)/shard_map/while
  300.0 1.7 copy-start
  326.3 11.9 %copy-start.1 = (bf16[32,256,128]{2,1,0:T(8,128)(2,1)S(1)}, bf16[32,256,128]{2,1,0:T(8,128)(2,1)}, u32[]{:S(2)}) copy-start(bf16[32,256,128]{2,1,0:T(8,128)(2,1)} %copy-done) | copy-start | bytes 6291460 | tf_op jit(solution)/shard_map/while
  449.7 13.9 %all-to-all-start.2 = ((f32[32,1,256]{2,1,0:T(1,128)}), f32[32,1,256]{2,1,0:T(1,128)S(1)}, u32[]{:S(2)}, u32[]{:S(2)}) async-start(f32[32,1,256]{2,1,0:T(1,128)} %all_to_all.16), calls=%async_computation.2 | async-start | bytes 65536 | tf_op jit(solution)/shard_map/all_to_all | solution.py:92
Sparse Core Ops, SparseCore 0:
  449.2 114.5 all-reduce.3
where the time goes:
time: 575 us; the launch traced here: 573 us
  blocking collectives  245 us (43%)
  waiting for transfers between devices  106 us (18%)
  matrix products  85.3 us (15%)
  local copies, waits for them, and re-layouts  62.9 us (11%)
  other arithmetic  42.1 us (7%)
  between operations  14.9 us (3%)
  starting transfers between devices  14.2 us (2%)
    unnamed x1, blocking collectives  108 us
    all_to_all x1, blocking collectives, shards(): lax.all_to_all(sum_acc, 'blk', split_axis=0, concat_axis=0, tiled=True)  99.4 us
    psum x1, waiting for transfers between devices, finish_sums(): total_sums, total_counts = lax.psum((own_sums, own_counts), 'slab')  61.6 us
    dot_general x4, matrix products, accumulate(): jnp.einsum('ns,ncd->scd', one_hot, partial_value.reshape(-1, CENT_BLK, EM...  45.1 us
    psum x1, blocking collectives, finish_sums(): total_sums, total_counts = lax.psum((own_sums, own_counts), 'slab')  37.7 us
    all_to_all x1, waiting for transfers between devices, shards(): lax.all_to_all(replies, 'blk', split_axis=0, concat_axis=0, tiled=True)  37.2 us
    convert_element_type x4, local copies, waits for them, and re-layouts, accumulate(): weights.astype(jnp.bfloat16).reshape(group_size, TOK_BLK, 3, CENT_BLK)  34.5 us
    reduce_sum x4, other arithmetic, accumulate(): jnp.sum(weights.reshape(group_size, TOK_BLK, 3, CENT_BLK), axis=1)  19.8 us
  transfers between devices with their start and end apart: 3, of which 3 were waited for; matrix products, arithmetic and copies ran while one was open for 2% of the time, Pallas kernels for 0%

commit v1 on v0

v1 whole, which is shorter than its diff:
```python
import functools
import math

import jax
import jax.numpy as jnp
from jax import lax
from jax.experimental import pallas as pl
from jax.experimental.pallas import tpu as pltpu
from jax.sharding import PartitionSpec as P

EMBED_WIDTH = 128
CENT_BLK = 256
TOK_BLK = 256
BPO = 32
MSG_ROWS = CENT_BLK + 8

SOFTMAX_TEMP = 0.1
PRIOR_WEIGHT = 4.0
EPSILON = 1e-06
EXP2_SCALE = math.log2(math.e) / (EMBED_WIDTH * SOFTMAX_TEMP)
CONTRACT_LAST = (((1,), (1,)), ((), ()))


def unit_rows(values):
    widened = values.astype(jnp.float32)
    return widened * lax.rsqrt(jnp.mean(widened * widened, axis=-1, keepdims=True) + EPSILON)


def split_counts(totals_a, totals_b):
    row = lax.broadcasted_iota(jnp.int32, (8, EMBED_WIDTH), 0)
    heads = jnp.where(row % 2 == 0, totals_a, totals_b)
    rounded = heads.astype(jnp.bfloat16).astype(jnp.float32)
    tails = heads - rounded
    tile = jnp.where(row < 2, rounded, jnp.where(row < 4, tails, 0.0))
    return tile.astype(jnp.bfloat16)


def attend_kernel(per_step, slots, tok_ref, cent_ref, out_ref, acc_ref, cnt_ref):
    step = pl.program_id(0)

    @pl.when(step == 0)
    def _():
        acc_ref[...] = jnp.zeros_like(acc_ref)
        cnt_ref[...] = jnp.zeros_like(cnt_ref)

    for at in range(per_step):
        block = step * per_step + at
        tok = unit_rows(tok_ref[pl.ds(at * TOK_BLK, TOK_BLK), :]).astype(jnp.bfloat16)
        ids = [slots[block * 3 + k] for k in range(3)]
        exps = []
        total = None
        for k in range(3):
            scores = lax.dot_general(
                cent_ref[ids[k]], tok, CONTRACT_LAST, preferred_element_type=jnp.float32
            )
            grown = jnp.exp2(scores * EXP2_SCALE)
            exps.append(grown)
            part = jnp.sum(grown, axis=0, keepdims=True)
            total = part if total is None else total + part
        inverse = 1.0 / total
        for k in range(3):
            weights = exps[k] * inverse
            cnt_ref[ids[k]] += weights[:, :128] + weights[:, 128:]
            acc_ref[ids[k]] += jnp.dot(
                weights.astype(jnp.bfloat16), tok, preferred_element_type=jnp.float32
            )

    @pl.when(step == pl.num_programs(0) - 1)
    def _():
        ones = jnp.ones((8, EMBED_WIDTH), jnp.float32)

        def write(slot, carry):
            out_ref[slot, :CENT_BLK, :] = acc_ref[slot].astype(jnp.bfloat16)
            counts = lax.dot_general(
                ones, cnt_ref[slot], CONTRACT_LAST,
                preferred_element_type=jnp.float32, precision=lax.Precision.HIGHEST,
            )
            out_ref[slot, CENT_BLK:, :] = split_counts(counts[:, :128], counts[:, 128:])
            return carry

        lax.fori_loop(0, cnt_ref.shape[0], write, 0)


def attend(slots, tokens, fetched, per_step=4):
    owners = fetched.shape[0]
    blocks = tokens.shape[0] // TOK_BLK
    per_step = math.gcd(per_step, blocks)
    pairs = blocks * 3 * TOK_BLK * CENT_BLK
    return pl.pallas_call(
        functools.partial(attend_kernel, per_step),
        grid_spec=pltpu.PrefetchScalarGridSpec(
            num_scalar_prefetch=1,
            grid=(blocks // per_step,),
            in_specs=[
                pl.BlockSpec((per_step * TOK_BLK, EMBED_WIDTH), lambda i, s: (i, 0)),
                pl.BlockSpec(fetched.shape, lambda i, s: (0, 0, 0), pipeline_mode=pl.Buffered(1)),
            ],
            out_specs=pl.BlockSpec(
                (owners, MSG_ROWS, EMBED_WIDTH), lambda i, s: (0, 0, 0),
                pipeline_mode=pl.Buffered(1),
            ),
            scratch_shapes=[
                pltpu.VMEM((owners, CENT_BLK, EMBED_WIDTH), jnp.float32),
                pltpu.VMEM((owners, CENT_BLK, EMBED_WIDTH), jnp.float32),
            ],
        ),
        out_shape=jax.ShapeDtypeStruct((owners, MSG_ROWS, EMBED_WIDTH), jnp.bfloat16),
        compiler_params=pltpu.CompilerParams(vmem_limit_bytes=40 << 20),
        cost_estimate=pl.CostEstimate(
            flops=pairs * EMBED_WIDTH * 4, transcendentals=pairs,
            bytes_accessed=tokens.size * 2 + fetched.size * 4,
        ),
        name="attend",
    )(slots, tokens, fetched)


def collect_kernel(asked, back_ref, out_ref, acc_ref):
    acc_ref[...] = jnp.zeros_like(acc_ref)

    def add(source, carry):
        inner = asked[source]

        @pl.when(inner >= 0)
        def _():
            acc_ref[inner] += back_ref[source].astype(jnp.float32)

        return carry

    lax.fori_loop(0, back_ref.shape[0], add, 0)

    def write(inner, carry):
        out_ref[inner, :CENT_BLK, :] = acc_ref[inner, :CENT_BLK, :].astype(jnp.bfloat16)
        tile = acc_ref[inner, CENT_BLK:, :]
        totals = tile[0:2] + tile[2:4]
        out_ref[inner, CENT_BLK:, :] = split_counts(totals[0:1], totals[1:2])
        return carry

    lax.fori_loop(0, out_ref.shape[0], write, 0)


def collect(asked, back):
    shape = (BPO, MSG_ROWS, EMBED_WIDTH)
    return pl.pallas_call(
        collect_kernel,
        grid_spec=pltpu.PrefetchScalarGridSpec(
            num_scalar_prefetch=1,
            grid=(1,),
            in_specs=[pl.BlockSpec(back.shape, lambda i, s: (0, 0, 0), pipeline_mode=pl.Buffered(1))],
            out_specs=pl.BlockSpec(shape, lambda i, s: (0, 0, 0), pipeline_mode=pl.Buffered(1)),
            scratch_shapes=[pltpu.VMEM(shape, jnp.float32)],
        ),
        out_shape=jax.ShapeDtypeStruct(shape, jnp.bfloat16),
        compiler_params=pltpu.CompilerParams(vmem_limit_bytes=24 << 20),
        cost_estimate=pl.CostEstimate(
            flops=back.size, transcendentals=0, bytes_accessed=back.size * 4
        ),
        name="collect",
    )(asked, back)


def shards(tokens, listed, centroids):
    owner_count = lax.axis_size("blk")
    slab_count = lax.axis_size("slab")
    slab_index = lax.axis_index("slab")
    share_blocks = BPO // slab_count

    owner_ids = jnp.arange(owner_count, dtype=jnp.int32)
    group_of = listed // BPO
    inner_ids = listed % BPO
    matches = group_of[:, :, None] == owner_ids
    wanted = jnp.max(jnp.where(matches, inner_ids[:, :, None] + 1, 0), axis=(0, 1)) - 1
    asked_ids = lax.all_to_all(
        wanted.reshape(owner_count, 1), "blk", split_axis=0, concat_axis=0, tiled=True
    ).reshape(owner_count)

    cent_send = unit_rows(centroids).astype(jnp.bfloat16).reshape(BPO, CENT_BLK, EMBED_WIDTH)
    replies = cent_send[jnp.maximum(asked_ids, 0)]
    fetched = lax.all_to_all(replies, "blk", split_axis=0, concat_axis=0, tiled=True)

    partial = attend(group_of.reshape(-1), tokens, fetched)
    back = lax.all_to_all(partial, "blk", split_axis=0, concat_axis=0, tiled=True)
    own = collect(asked_ids, back)
    slabs = lax.all_to_all(own, "slab", split_axis=0, concat_axis=0, tiled=True)
    slabs = slabs.reshape(slab_count, share_blocks, MSG_ROWS, EMBED_WIDTH)

    totals = jnp.sum(slabs.astype(jnp.float32), axis=0)
    counts = (totals[:, CENT_BLK:CENT_BLK + 2] + totals[:, CENT_BLK + 2:CENT_BLK + 4]).reshape(-1)
    sums = totals[:, :CENT_BLK].reshape(-1, EMBED_WIDTH)
    rows = share_blocks * CENT_BLK
    mine = unit_rows(lax.dynamic_slice_in_dim(centroids, slab_index * rows, rows, 0))
    refined = (sums + PRIOR_WEIGHT * mine) / (counts[:, None] + PRIOR_WEIGHT)
    return refined, counts


def solution(mesh):
    placed = (P(("blk", "slab"), None), P(("blk", "slab"), None), P("blk", None))
    return jax.shard_map(
        shards,
        mesh=mesh,
        in_specs=placed,
        out_specs=(P(("blk", "slab"), None), P(("blk", "slab"))),
        check_vma=False,
    )
```

time: 575 us -> 221 us (0.38)
  blocking collectives: 245 us -> 58.4 us
  matrix products: 85.3 us -> 0 us
  local copies, waits for them, and re-layouts: 62.9 us -> 6.86 us
  Pallas kernels: 0 us -> 42.7 us
  other arithmetic: 42.1 us -> 10.8 us
  waiting for transfers between devices: 106 us -> 77.5 us
  between operations: 14.9 us -> 0.74 us
  starting transfers between devices: 14.2 us -> 23 us
    unnamed x1 -> x0, blocking collectives: 108 us -> none
    dot_general x18 -> x0, matrix products: 85.3 us -> none  [the longest x4 45.1 us: accumulate(): jnp.einsum('ns,ncd->scd', one_hot, partial_value.reshape(-1, CENT_BLK, EM...]
    psum x1 -> x0, waiting for transfers between devices: 61.6 us -> none  [finish_sums(): total_sums, total_counts = lax.psum((own_sums, own_counts), 'slab')]
    pallas_call x0 -> x2, Pallas kernels: none -> 42.7 us  [the longest x1 39.3 us: attend(): pl.pallas_call(functools.partial(attend_kernel, per_step), grid_spec=pltp...]
    all_to_all x1, blocking collectives: 99.4 us -> 58.4 us  [shards(): lax.all_to_all(partial, 'blk', split_axis=0, concat_axis=0, tiled=True)]
    psum x1 -> x0, blocking collectives: 37.7 us -> none  [finish_sums(): total_sums, total_counts = lax.psum((own_sums, own_counts), 'slab')]
    convert_element_type x4 -> x0, local copies, waits for them, and re-layouts: 34.5 us -> none  [accumulate(): weights.astype(jnp.bfloat16).reshape(group_size, TOK_BLK, 3, CENT_BLK)]
    all_to_all x1 -> x2, waiting for transfers between devices: 6.85 us -> 28.4 us  [the longest x1 25.7 us: shards(): slabs = lax.all_to_all(own, 'slab', split_axis=0, concat_axis=0, tiled=True)]
  transfers between devices with their start and end apart: 3 -> 3, of which waited for: 3 -> 3; matrix products, arithmetic and copies ran while one was open for 2% -> 3% of each run, Pallas kernels for 0% -> 0%
where the time goes in v1:
time: 221 us; the launch traced here: 220 us
  waiting for transfers between devices  77.5 us (35%)
  blocking collectives  58.4 us (26%)
  Pallas kernels  42.7 us (19%)
  starting transfers between devices  23 us (10%)
  other arithmetic  10.8 us (5%)
  local copies, waits for them, and re-layouts  6.86 us (3%)
    all_to_all x1, blocking collectives, shards(): lax.all_to_all(partial, 'blk', split_axis=0, concat_axis=0, tiled=True)  58.4 us
    all_to_all x1, waiting for transfers between devices, shards(): lax.all_to_all(replies, 'blk', split_axis=0, concat_axis=0, tiled=True)  49 us
    pallas_call x1, Pallas kernels, attend(): pl.pallas_call(functools.partial(attend_kernel, per_step), grid_spec=pltp...  39.3 us
    all_to_all x1, waiting for transfers between devices, shards(): slabs = lax.all_to_all(own, 'slab', split_axis=0, concat_axis=0, tiled=True)  25.7 us
    all_to_all x1, starting transfers between devices, shards(): lax.all_to_all(wanted.reshape(owner_count, 1), 'blk', split_axis=0, conca...  11 us
    all_to_all x1, starting transfers between devices, shards(): slabs = lax.all_to_all(own, 'slab', split_axis=0, concat_axis=0, tiled=True)  6.38 us
    all_to_all x1, starting transfers between devices, shards(): lax.all_to_all(replies, 'blk', split_axis=0, concat_axis=0, tiled=True)  5.6 us
  transfers between devices with their start and end apart: 3, of which 3 were waited for; matrix products, arithmetic and copies ran while one was open for 3% of the time, Pallas kernels for 0%

profile of v1, /device:TPU:1, one launch (start us, length us, event | category | flops | bytes accessed | tf_op | source)
XLA Modules:
  0.0 220.0 jit_solution(5767820486264000959)
XLA Ops:
  0.6 0.0 copy-start.1
  0.6 0.8 add_select_fusion.1
  1.5 0.1 select_reduce_fusion
  1.6 0.7 copy.18
  2.3 11.0 %all-to-all-start = ((s32[32,1,1]{2,1,0:T(1,128)}), s32[32,1,1]{2,1,0:T(1,128)S(1)}, u32[]{:S(2)}, u32[]{:S(2)}) async-start(s32[32,1,1]{2,1,0:T(1,128)} %copy.18), calls=%async_computation | async-start | bytes 32768 | tf_op jit(solution)/shard_map/all_to_all | solution.py:172
  13.4 2.7 %fusion = f32[8192]{0:T(1024)S(1)} fusion(bf16[8192,128]{1,0:T(8,128)(2,1)} %param.5), kind=kLoop, calls=%fused_computation.4 | loop fusion | flops 3137536 | bytes 2129920 | tf_op jit(solution)/shard_map/reduce_sum | solution.py:26
  16.1 0.0 copy-done.1
  16.1 2.3 %fusion.1 = bf16[8192,128]{1,0:T(8,128)(2,1)} fusion(bf16[8192,128]{1,0:T(8,128)(2,1)S(1)} %copy-done.1, f32[8192]{0:T(1024)S(1)} %add_rsqrt_fusion), kind=kLoop, calls=%fused_computation.5 | loop fusion | flops 3145728 | bytes 4227072 | tf_op jit(solution)/shard_map/convert_element_type | solution.py:176
  18.4 2.7 %all-to-all-done = s32[32,1,1]{2,1,0:T(1,128)S(1)} async-done(((s32[32,1,1]{2,1,0:T(1,128)}), s32[32,1,1]{2,1,0:T(1,128)S(1)}, u32[]{:S(2)}, u32[]{:S(2)}) %all-to-all-start) | async-done | bytes 160 | tf_op jit(solution)/shard_map/all_to_all | solution.py:172
  21.1 1.2 maximum_reduce_fusion
  22.4 3.7 %gather_fusion = bf16[32,256,128]{2,1,0:T(8,128)(2,1)} fusion(bf16[32,256,128]{2,1,0:T(8,128)(2,1)} %bitcast.9, s32[1024]{0:T(1024)S(1)} %pad_clamp_fusion), kind=kCustom, calls=%fused_computation | custom fusion | bytes 4194432 | tf_op jit(solution)/shard_map/gather | solution.py:177
  26.1 5.6 %all-to-all-start.1 = ((bf16[32,256,128]{2,1,0:T(8,128)(2,1)}), bf16[32,256,128]{2,1,0:T(8,128)(2,1)S(1)}, u32[]{:S(2)}, u32[]{:S(2)}) async-start(bf16[32,256,128]{2,1,0:T(8,128)(2,1)} %gather_fusion), calls=%async_computation.1 | async-start | bytes 4194304 | tf_op jit(solution)/shard_map/all_to_all | solution.py:178
  31.7 0.1 copy.19
  31.8 0.1 reshape.72.slots
  31.9 49.0 %all-to-all-done.1.cent_ref = bf16[32,256,128]{2,1,0:T(8,128)(2,1)S(1)} async-done(((bf16[32,256,128]{2,1,0:T(8,128)(2,1)}), bf16[32,256,128]{2,1,0:T(8,128)(2,1)S(1)}, u32[]{:S(2)}, u32[]{:S(2)}) %all-to-all-start.1) | async-done | bytes 2097184 | tf_op jit(solution)/shard_map/all_to_all | solution.py:178
  80.9 0.0 copy-start
  80.9 2.2 copy-done
  83.1 39.3 %attend.1 = bf16[32,264,128]{2,1,0:T(8,128)(2,1)S(1)} custom-call(s32[192]{0:T(256)S(1)} %reshape.72.slots, bf16[16384,128]{1,0:T(8,128)(2,1)S(1)} %copy-done, bf16[32,256,128]{2,1,0:T(8,128)(2,1)S(1)} %all-to-all-done.1.cent_ref), custom_call_target="tpu_custom_call" | custom-call | flops 6442450944 | bytes 8388608 | tf_op jit(solution)/shard_map/attend/pallas_call | solution.py:89
  122.4 58.4 %all_to_all.21.back_ref = bf16[32,264,128]{2,1,0:T(8,128)(2,1)S(1)} all-to-all(bf16[32,264,128]{2,1,0:T(8,128)(2,1)S(1)} %attend.1), channel_id=1, replica_groups=mesh['blk'=32,'slab'=8] {'blk'}, dimensions={0} | all-to-all | bytes 4325376 | tf_op jit(solution)/shard_map/all_to_all | solution.py:181
  180.8 3.4 %collect.1 = bf16[32,264,128]{2,1,0:T(8,128)(2,1)} custom-call(s32[32]{0:T(128)S(1)} %get-tuple-element.3.asked, bf16[32,264,128]{2,1,0:T(8,128)(2,1)S(1)} %all_to_all.21.back_ref), custom_call_target="tpu_custom_call" | custom-call | flops 1081344 | bytes 4325376 | tf_op jit(solution)/shard_map/collect/pallas_call | solution.py:143
  184.2 6.4 %all-to-all-start.3 = ((bf16[32,264,128]{2,1,0:T(8,128)(2,1)}), bf16[32,264,128]{2,1,0:T(8,128)(2,1)S(1)}, u32[]{:S(2)}, u32[]{:S(2)}) async-start(bf16[32,264,128]{2,1,0:T(8,128)(2,1)} %collect.1), calls=%async_computation.3 | async-start | bytes 4325376 | tf_op jit(solution)/shard_map/all_to_all | solution.py:183
  190.6 1.2 fusion.2
  191.8 25.7 %all-to-all-done.3 = bf16[32,264,128]{2,1,0:T(8,128)(2,1)S(1)} async-done(((bf16[32,264,128]{2,1,0:T(8,128)(2,1)}), bf16[32,264,128]{2,1,0:T(8,128)(2,1)S(1)}, u32[]{:S(2)}, u32[]{:S(2)}) %all-to-all-start.3) | async-done | bytes 2162720 | tf_op jit(solution)/shard_map/all_to_all | solution.py:183
  217.5 0.3 convert_reduce_fusion
  217.8 0.0 copy-start.2
  217.9 2.1 fusion.5
  220.0 0.0 copy-done.2
  (7 shorter events, 0.1 us)
Async XLA Ops:
  0.6 15.5 %copy-start.1 = (bf16[8192,128]{1,0:T(8,128)(2,1)S(1)}, bf16[8192,128]{1,0:T(8,128)(2,1)}, u32[]{:S(2)}) copy-start(bf16[8192,128]{1,0:T(8,128)(2,1)} %param.5) | copy-start | bytes 6291460
  2.3 18.8 %all-to-all-start = ((s32[32,1,1]{2,1,0:T(1,128)}), s32[32,1,1]{2,1,0:T(1,128)S(1)}, u32[]{:S(2)}, u32[]{:S(2)}) async-start(s32[32,1,1]{2,1,0:T(1,128)} %copy.18), calls=%async_computation | async-start | bytes 32768 | tf_op jit(solution)/shard_map/all_to_all | solution.py:172
  26.1 54.9 %all-to-all-start.1 = ((bf16[32,256,128]{2,1,0:T(8,128)(2,1)}), bf16[32,256,128]{2,1,0:T(8,128)(2,1)S(1)}, u32[]{:S(2)}, u32[]{:S(2)}) async-start(bf16[32,256,128]{2,1,0:T(8,128)(2,1)} %gather_fusion), calls=%async_computation.1 | async-start | bytes 4194304 | tf_op jit(solution)/shard_map/all_to_all | solution.py:178
  80.9 2.2 copy-start
  184.2 33.3 %all-to-all-start.3 = ((bf16[32,264,128]{2,1,0:T(8,128)(2,1)}), bf16[32,264,128]{2,1,0:T(8,128)(2,1)S(1)}, u32[]{:S(2)}, u32[]{:S(2)}) async-start(bf16[32,264,128]{2,1,0:T(8,128)(2,1)} %collect.1), calls=%async_computation.3 | async-start | bytes 4325376 | tf_op jit(solution)/shard_map/all_to_all | solution.py:183
  217.8 2.2 copy-start.2
